TPU v7x, 256 devices: a whole 4x4x8 slice. The times are simulated.
256 devices in a mesh: section: 2 (over core), ctx: 128 (over y, z, x).
Axes of the slice: x: 4, y: 4, z: 8, core: 2. Of those that a mesh axis runs over, the one named last changes fastest.
Arguments:
- queries: bfloat16 [2, 8192, 4096], P('section', 'ctx'), may hold values from -80 to 80
- key_rows: bfloat16 [2, 8192, 512], P('section', 'ctx'), may hold values from -8 to 8
- rows_of_value: bfloat16 [2, 8192, 512], P('section', 'ctx'), may hold values from -6 to 6
- query_gain: float32 [4096], replicated, may hold values from 2 to 6
- block_order: int32 [256], replicated, may hold values from 0 to 255, each once
Outputs:
- attended: bfloat16 [2, 8192, 4096], P('section', 'ctx')
Inputs may be any that keep to these rules, and one draw needn't show every extreme that they name: A permutation; stored block j of 32 rows holds the sequence's block block_order[j].
All inputs are finite; a program needn't handle non-finite values.
Results may differ from a plain program's by a relative error of at most 0.0085.
Values may be sent and summed in bfloat16 or wider, within the bound.
A program may use at most 192 MiB of HBM per device.

v0:
```python
import math

import jax
import jax.numpy as jnp
from jax import lax
from jax.sharding import PartitionSpec as P

HEAD_SIZE = 128
QUERY_PER_GROUP = 8


def from_behind(value, axis, steps):
    count = lax.axis_size(axis)
    initial, last = (max(0, -steps), min(count, count - steps))
    return lax.ppermute(value, axis, [(source, source + steps) for source in range(initial, last)])


def key_positions(block_order, first_row_index, row_count, block_rows):
    row_ids = first_row_index + jnp.arange(row_count, dtype=jnp.int32)
    slot_ids = row_ids // block_rows
    slot_table = jnp.arange(block_order.shape[0], dtype=jnp.int32)
    picked = jnp.sum(
        jnp.where(slot_ids[:, None] == slot_table[None, :], block_order[None, :], 0), axis=1
    )
    return picked * block_rows + row_ids % block_rows


def fold_step(carry_state, key_piece, value_piece, key_pos, query_four, query_pos, needed):
    row_count = key_piece.shape[0]
    kv_heads = query_four.shape[1]
    score_scale = 1.0 / math.sqrt(HEAD_SIZE)

    def compute(old_state):
        row_max, row_sum, mixed_sum = old_state
        key_quad = key_piece.reshape(row_count, kv_heads, HEAD_SIZE)
        scores = (
            jnp.einsum("qjgd,kjd->jgqk", query_four, key_quad, preferred_element_type=jnp.float32)
            * score_scale
        )
        scores = jnp.where(key_pos[None, :] <= query_pos[:, None], scores, -jnp.inf)
        new_max = jnp.maximum(row_max, jnp.max(scores, axis=-1))
        rescale = jnp.exp(row_max - new_max)
        weights = jnp.exp(scores - new_max[..., None])
        new_sum = row_sum * rescale + jnp.sum(weights, axis=-1)
        value_four = value_piece.reshape(row_count, kv_heads, HEAD_SIZE)
        product = jnp.einsum(
            "jgqk,kjd->qjgd",
            weights.astype(jnp.bfloat16),
            value_four,
            preferred_element_type=jnp.float32,
        )
        new_mixed = mixed_sum * jnp.transpose(rescale, (2, 0, 1))[..., None] + product
        return (new_max, new_sum, new_mixed)

    return lax.cond(needed, compute, lambda same_state: same_state, carry_state)


def body(queries, key_rows, rows_of_value, query_gain, block_order):
    rows_here = queries.shape[1]
    block_rows = rows_here // 2
    query_pos = key_positions(block_order, lax.axis_index("ctx") * rows_here, rows_here, block_rows)
    section_now = lax.axis_index("section")
    kv_heads = key_rows.shape[2] // HEAD_SIZE
    column_count = queries.shape[2]
    start_state = (
        jnp.full((kv_heads, QUERY_PER_GROUP, rows_here), -1e30, jnp.float32),
        jnp.zeros((kv_heads, QUERY_PER_GROUP, rows_here), jnp.float32),
        jnp.zeros((rows_here, kv_heads, QUERY_PER_GROUP, HEAD_SIZE), jnp.float32),
    )

    def finish(final_state):
        row_max, row_sum, mixed_sum = final_state
        safe_sum = jnp.where(row_sum > 0.0, row_sum, 1.0)
        mixed_out = mixed_sum / jnp.transpose(safe_sum, (2, 0, 1))[..., None]
        return mixed_out.reshape(rows_here, column_count).astype(jnp.bfloat16)

    gathered = (
        lax.all_gather(key_rows, "ctx", axis=1, tiled=True),
        lax.all_gather(rows_of_value, "ctx", axis=1, tiled=True),
    )
    total_rows = gathered[0].shape[1]
    width_of_block = math.gcd(total_rows, 512)

    def attend(rows_of_query, active):
        query_four = rows_of_query.reshape(rows_here, kv_heads, QUERY_PER_GROUP, HEAD_SIZE)

        def loop_body(loop_index, carry_state):
            first_row_index = loop_index * width_of_block
            key_piece = lax.dynamic_slice_in_dim(gathered[0][0], first_row_index, width_of_block, 0)
            value_piece = lax.dynamic_slice_in_dim(
                gathered[1][0], first_row_index, width_of_block, 0
            )
            key_pos = key_positions(block_order, first_row_index, width_of_block, block_rows)
            return fold_step(
                carry_state, key_piece, value_piece, key_pos, query_four, query_pos, active
            )

        return finish(lax.fori_loop(0, total_rows // width_of_block, loop_body, start_state))

    first_out = attend(queries[0], section_now == 0)
    received = from_behind(first_out, "section", 1)
    shifted = (
        queries[0].astype(jnp.float32) + query_gain[None, :] * received.astype(jnp.float32)
    ).astype(jnp.bfloat16)
    second = attend(shifted, section_now == 1)
    result = jnp.where(section_now == 0, first_out, second)
    return result[None]


def solution(mesh):
    placed = (
        P("section", "ctx", None),
        P("section", "ctx", None),
        P("section", "ctx", None),
        P(),
        P(),
    )
    return jax.shard_map(
        body, mesh=mesh, in_specs=placed, out_specs=P("section", "ctx", None), check_vma=False
    )
```

profile of v0, /device:TPU:1, one launch (start us, length us, event | category | flops | bytes accessed | tf_op | source)
XLA Modules:
  0.0 462.5 jit_solution(13137162699228120019)
XLA Ops:
  10.3 125.7 %all-gather.3.cloned.1.call-done = bf16[1,8192,512]{2,1,0:T(8,128)(2,1)} async-done(((bf16[1,64,512]{2,1,0:T(8,128)(2,1)}), bf16[1,8192,512]{2,1,0:T(8,128)(2,1)}) %all-gather.3.cloned.1.call-update) | async-done | bytes 8388624 | tf_op jit(solution)/shard_map/all_gather | solution.py:78
  135.9 12.0 %copy.33 = bf16[1,8192,512]{1,2,0:T(8,128)(2,1)} copy(bf16[1,8192,512]{2,1,0:T(8,128)(2,1)} %all-gather.3.cloned.1.call-done) | data formatting | bytes 16777216 | tf_op jit(solution)/shard_map/while | solution.py:98
  147.9 112.4 %all-gather.5.cloned.1.call-done = bf16[1,8192,512]{2,1,0:T(8,128)(2,1)} async-done(((bf16[1,64,512]{2,1,0:T(8,128)(2,1)}), bf16[1,8192,512]{2,1,0:T(8,128)(2,1)}) %all-gather.5.cloned.1.call-update) | async-done | bytes 8388624 | tf_op jit(solution)/shard_map/all_gather | solution.py:79
  260.3 11.9 %copy.35 = bf16[1,8192,512]{1,2,0:T(8,128)(2,1)} copy(bf16[1,8192,512]{2,1,0:T(8,128)(2,1)} %all-gather.5.cloned.1.call-done) | data formatting | bytes 16777216 | tf_op jit(solution)/shard_map/while | solution.py:98
  272.4 1.7 while.38
  275.1 1.5 collective-permute-start
  276.6 89.6 %collective-permute-done = bf16[64,4096]{1,0:T(8,128)(2,1)S(1)} collective-permute-done((bf16[64,4096]{1,0:T(8,128)(2,1)S(1)}, bf16[64,4096]{1,0:T(8,128)(2,1)S(1)}, u32[]{:S(2)}, u32[]{:S(2)}) %collective-permute-start) | collective-permute-done | bytes 524320 | tf_op jit(solution)/shard_map/ppermute | solution.py:15
  366.7 86.8 %while.39 = (s32[]{:T(128)}, f32[4,8,64]{2,1,0:T(8,128)S(1)}, f32[4,8,64]{2,1,0:T(8,128)S(1)}, f32[64,4,8,128]{3,0,2,1:T(8,128)S(1)}, pred[]{:T(512)}, /*index=5...) while((s32[]{:T(128)}, f32[4,8,64]{2,1,0:T(8,128)S(1)}, ...), condition=%wide.region_14.15_spmd, body=%wide.region_8.14_spmd.sunk | while | flops 549376512 | bytes 19682900 | solution.py:98
  366.8 5.3 %conditional.5 = ((f32[4,8,64]{2,1,0:T(8,128)S(1)}, f32[4,8,64]{2,1,0:T(8,128)S(1)}, f32[64,4,8,128]{3,0,2,1:T(8,128)S(1)})) conditional(s32[]{:T(128)} %convert_element_type.110, (f32[4,8,64]{2,1,0:T(8,128)S(1)}, f32[4,8,64]{2,1,0:T(8,128)S(1)}, f32[64,4,8,128]{3,0,2,1:T(8,128)S(1)}) %tuple.209, (s32[]{:T(128)}, ...), branch_computations={%region_9.9_spmd, %region_10.13_spmd.clone.clone} | conditional | flops 549376512 | bytes 19154254 | solution.py:55
  369.3 1.5 fusion.32
  370.8 1.3 fusion.21
  372.3 5.3 %conditional.5 = ((f32[4,8,64]{2,1,0:T(8,128)S(1)}, f32[4,8,64]{2,1,0:T(8,128)S(1)}, f32[64,4,8,128]{3,0,2,1:T(8,128)S(1)})) conditional(s32[]{:T(128)} %convert_element_type.110, (f32[4,8,64]{2,1,0:T(8,128)S(1)}, f32[4,8,64]{2,1,0:T(8,128)S(1)}, f32[64,4,8,128]{3,0,2,1:T(8,128)S(1)}) %tuple.209, (s32[]{:T(128)}, ...), branch_computations={%region_9.9_spmd, %region_10.13_spmd.clone.clone} | conditional | flops 549376512 | bytes 19154254 | solution.py:55
  374.7 1.5 fusion.32
  376.3 1.3 fusion.21
  377.7 5.3 %conditional.5 = ((f32[4,8,64]{2,1,0:T(8,128)S(1)}, f32[4,8,64]{2,1,0:T(8,128)S(1)}, f32[64,4,8,128]{3,0,2,1:T(8,128)S(1)})) conditional(s32[]{:T(128)} %convert_element_type.110, (f32[4,8,64]{2,1,0:T(8,128)S(1)}, f32[4,8,64]{2,1,0:T(8,128)S(1)}, f32[64,4,8,128]{3,0,2,1:T(8,128)S(1)}) %tuple.209, (s32[]{:T(128)}, ...), branch_computations={%region_9.9_spmd, %region_10.13_spmd.clone.clone} | conditional | flops 549376512 | bytes 19154254 | solution.py:55
  380.2 1.5 fusion.32
  381.7 1.3 fusion.21
  383.1 5.3 %conditional.5 = ((f32[4,8,64]{2,1,0:T(8,128)S(1)}, f32[4,8,64]{2,1,0:T(8,128)S(1)}, f32[64,4,8,128]{3,0,2,1:T(8,128)S(1)})) conditional(s32[]{:T(128)} %convert_element_type.110, (f32[4,8,64]{2,1,0:T(8,128)S(1)}, f32[4,8,64]{2,1,0:T(8,128)S(1)}, f32[64,4,8,128]{3,0,2,1:T(8,128)S(1)}) %tuple.209, (s32[]{:T(128)}, ...), branch_computations={%region_9.9_spmd, %region_10.13_spmd.clone.clone} | conditional | flops 549376512 | bytes 19154254 | solution.py:55
  385.6 1.5 fusion.32
  387.1 1.3 fusion.21
  388.5 5.3 %conditional.5 = ((f32[4,8,64]{2,1,0:T(8,128)S(1)}, f32[4,8,64]{2,1,0:T(8,128)S(1)}, f32[64,4,8,128]{3,0,2,1:T(8,128)S(1)})) conditional(s32[]{:T(128)} %convert_element_type.110, (f32[4,8,64]{2,1,0:T(8,128)S(1)}, f32[4,8,64]{2,1,0:T(8,128)S(1)}, f32[64,4,8,128]{3,0,2,1:T(8,128)S(1)}) %tuple.209, (s32[]{:T(128)}, ...), branch_computations={%region_9.9_spmd, %region_10.13_spmd.clone.clone} | conditional | flops 549376512 | bytes 19154254 | solution.py:55
  391.0 1.5 fusion.32
  392.5 1.3 fusion.21
  394.0 5.3 %conditional.5 = ((f32[4,8,64]{2,1,0:T(8,128)S(1)}, f32[4,8,64]{2,1,0:T(8,128)S(1)}, f32[64,4,8,128]{3,0,2,1:T(8,128)S(1)})) conditional(s32[]{:T(128)} %convert_element_type.110, (f32[4,8,64]{2,1,0:T(8,128)S(1)}, f32[4,8,64]{2,1,0:T(8,128)S(1)}, f32[64,4,8,128]{3,0,2,1:T(8,128)S(1)}) %tuple.209, (s32[]{:T(128)}, ...), branch_computations={%region_9.9_spmd, %region_10.13_spmd.clone.clone} | conditional | flops 549376512 | bytes 19154254 | solution.py:55
  396.4 1.5 fusion.32
  397.9 1.3 fusion.21
  399.4 5.3 %conditional.5 = ((f32[4,8,64]{2,1,0:T(8,128)S(1)}, f32[4,8,64]{2,1,0:T(8,128)S(1)}, f32[64,4,8,128]{3,0,2,1:T(8,128)S(1)})) conditional(s32[]{:T(128)} %convert_element_type.110, (f32[4,8,64]{2,1,0:T(8,128)S(1)}, f32[4,8,64]{2,1,0:T(8,128)S(1)}, f32[64,4,8,128]{3,0,2,1:T(8,128)S(1)}) %tuple.209, (s32[]{:T(128)}, ...), branch_computations={%region_9.9_spmd, %region_10.13_spmd.clone.clone} | conditional | flops 549376512 | bytes 19154254 | solution.py:55
  401.8 1.5 fusion.32
  404.8 5.3 %conditional.5 = ((f32[4,8,64]{2,1,0:T(8,128)S(1)}, f32[4,8,64]{2,1,0:T(8,128)S(1)}, f32[64,4,8,128]{3,0,2,1:T(8,128)S(1)})) conditional(s32[]{:T(128)} %convert_element_type.110, (f32[4,8,64]{2,1,0:T(8,128)S(1)}, f32[4,8,64]{2,1,0:T(8,128)S(1)}, f32[64,4,8,128]{3,0,2,1:T(8,128)S(1)}) %tuple.209, (s32[]{:T(128)}, ...), branch_computations={%region_9.9_spmd, %region_10.13_spmd.clone.clone} | conditional | flops 549376512 | bytes 19154254 | solution.py:55
  407.3 1.5 fusion.32
  410.2 5.3 %conditional.5 = ((f32[4,8,64]{2,1,0:T(8,128)S(1)}, f32[4,8,64]{2,1,0:T(8,128)S(1)}, f32[64,4,8,128]{3,0,2,1:T(8,128)S(1)})) conditional(s32[]{:T(128)} %convert_element_type.110, (f32[4,8,64]{2,1,0:T(8,128)S(1)}, f32[4,8,64]{2,1,0:T(8,128)S(1)}, f32[64,4,8,128]{3,0,2,1:T(8,128)S(1)}) %tuple.209, (s32[]{:T(128)}, ...), branch_computations={%region_9.9_spmd, %region_10.13_spmd.clone.clone} | conditional | flops 549376512 | bytes 19154254 | solution.py:55
  412.7 1.5 fusion.32
  414.2 1.3 fusion.21
  415.6 5.3 %conditional.5 = ((f32[4,8,64]{2,1,0:T(8,128)S(1)}, f32[4,8,64]{2,1,0:T(8,128)S(1)}, f32[64,4,8,128]{3,0,2,1:T(8,128)S(1)})) conditional(s32[]{:T(128)} %convert_element_type.110, (f32[4,8,64]{2,1,0:T(8,128)S(1)}, f32[4,8,64]{2,1,0:T(8,128)S(1)}, f32[64,4,8,128]{3,0,2,1:T(8,128)S(1)}) %tuple.209, (s32[]{:T(128)}, ...), branch_computations={%region_9.9_spmd, %region_10.13_spmd.clone.clone} | conditional | flops 549376512 | bytes 19154254 | solution.py:55
  418.1 1.5 fusion.32
  419.6 1.3 fusion.21
  421.1 5.3 %conditional.5 = ((f32[4,8,64]{2,1,0:T(8,128)S(1)}, f32[4,8,64]{2,1,0:T(8,128)S(1)}, f32[64,4,8,128]{3,0,2,1:T(8,128)S(1)})) conditional(s32[]{:T(128)} %convert_element_type.110, (f32[4,8,64]{2,1,0:T(8,128)S(1)}, f32[4,8,64]{2,1,0:T(8,128)S(1)}, f32[64,4,8,128]{3,0,2,1:T(8,128)S(1)}) %tuple.209, (s32[]{:T(128)}, ...), branch_computations={%region_9.9_spmd, %region_10.13_spmd.clone.clone} | conditional | flops 549376512 | bytes 19154254 | solution.py:55
  423.5 1.5 fusion.32
  426.5 5.3 %conditional.5 = ((f32[4,8,64]{2,1,0:T(8,128)S(1)}, f32[4,8,64]{2,1,0:T(8,128)S(1)}, f32[64,4,8,128]{3,0,2,1:T(8,128)S(1)})) conditional(s32[]{:T(128)} %convert_element_type.110, (f32[4,8,64]{2,1,0:T(8,128)S(1)}, f32[4,8,64]{2,1,0:T(8,128)S(1)}, f32[64,4,8,128]{3,0,2,1:T(8,128)S(1)}) %tuple.209, (s32[]{:T(128)}, ...), branch_computations={%region_9.9_spmd, %region_10.13_spmd.clone.clone} | conditional | flops 549376512 | bytes 19154254 | solution.py:55
  429.0 1.5 fusion.32
  431.9 5.3 %conditional.5 = ((f32[4,8,64]{2,1,0:T(8,128)S(1)}, f32[4,8,64]{2,1,0:T(8,128)S(1)}, f32[64,4,8,128]{3,0,2,1:T(8,128)S(1)})) conditional(s32[]{:T(128)} %convert_element_type.110, (f32[4,8,64]{2,1,0:T(8,128)S(1)}, f32[4,8,64]{2,1,0:T(8,128)S(1)}, f32[64,4,8,128]{3,0,2,1:T(8,128)S(1)}) %tuple.209, (s32[]{:T(128)}, ...), branch_computations={%region_9.9_spmd, %region_10.13_spmd.clone.clone} | conditional | flops 549376512 | bytes 19154254 | solution.py:55
  434.4 1.5 fusion.32
  437.3 5.3 %conditional.5 = ((f32[4,8,64]{2,1,0:T(8,128)S(1)}, f32[4,8,64]{2,1,0:T(8,128)S(1)}, f32[64,4,8,128]{3,0,2,1:T(8,128)S(1)})) conditional(s32[]{:T(128)} %convert_element_type.110, (f32[4,8,64]{2,1,0:T(8,128)S(1)}, f32[4,8,64]{2,1,0:T(8,128)S(1)}, f32[64,4,8,128]{3,0,2,1:T(8,128)S(1)}) %tuple.209, (s32[]{:T(128)}, ...), branch_computations={%region_9.9_spmd, %region_10.13_spmd.clone.clone} | conditional | flops 549376512 | bytes 19154254 | solution.py:55
  439.8 1.5 fusion.32
  442.8 5.3 %conditional.5 = ((f32[4,8,64]{2,1,0:T(8,128)S(1)}, f32[4,8,64]{2,1,0:T(8,128)S(1)}, f32[64,4,8,128]{3,0,2,1:T(8,128)S(1)})) conditional(s32[]{:T(128)} %convert_element_type.110, (f32[4,8,64]{2,1,0:T(8,128)S(1)}, f32[4,8,64]{2,1,0:T(8,128)S(1)}, f32[64,4,8,128]{3,0,2,1:T(8,128)S(1)}) %tuple.209, (s32[]{:T(128)}, ...), branch_computations={%region_9.9_spmd, %region_10.13_spmd.clone.clone} | conditional | flops 549376512 | bytes 19154254 | solution.py:55
  445.2 1.5 fusion.32
  448.2 5.3 %conditional.5 = ((f32[4,8,64]{2,1,0:T(8,128)S(1)}, f32[4,8,64]{2,1,0:T(8,128)S(1)}, f32[64,4,8,128]{3,0,2,1:T(8,128)S(1)})) conditional(s32[]{:T(128)} %convert_element_type.110, (f32[4,8,64]{2,1,0:T(8,128)S(1)}, f32[4,8,64]{2,1,0:T(8,128)S(1)}, f32[64,4,8,128]{3,0,2,1:T(8,128)S(1)}) %tuple.209, (s32[]{:T(128)}, ...), branch_computations={%region_9.9_spmd, %region_10.13_spmd.clone.clone} | conditional | flops 549376512 | bytes 19154254 | solution.py:55
  450.7 1.5 fusion.32
  (296 shorter events, 58.4 us)
Async XLA Ops:
  6.5 129.4 %all-gather.3.cloned.1.call-start = ((), (), s32[]{:S(2)}) async-start(), calls=%async_computation | async-start | bytes 8454144 | tf_op jit(solution)/shard_map/all_gather | solution.py:78
  7.3 253.0 %all-gather.5.cloned.1.call-start = ((), (), s32[]{:S(2)}) async-start(), calls=%async_computation.1 | async-start | bytes 8454144 | tf_op jit(solution)/shard_map/all_gather | solution.py:79
  147.9 124.5 %copy-start.1 = (s32[256]{0:T(256)S(1)}, s32[256]{0:T(256)}, u32[]{:S(2)}) copy-start(s32[256]{0:T(256)} %param.17) | copy-start | bytes 3076
  272.4 93.7 %copy-start = (bf16[1,64,4096]{2,1,0:T(8,128)(2,1)S(1)}, bf16[1,64,4096]{2,1,0:T(8,128)(2,1)}, u32[]{:S(2)}) copy-start(bf16[1,64,4096]{2,1,0:T(8,128)(2,1)} %param.13) | copy-start | bytes 1572868
  272.4 93.7 %copy-start.2 = (f32[4096]{0:T(1024)S(1)}, f32[4096]{0:T(1024)}, u32[]{:S(2)}) copy-start(f32[4096]{0:T(1024)} %param.16) | copy-start | bytes 49156
  275.1 91.0 %collective-permute-start = (bf16[64,4096]{1,0:T(8,128)(2,1)S(1)}, bf16[64,4096]{1,0:T(8,128)(2,1)S(1)}, u32[]{:S(2)}, u32[]{:S(2)}) collective-permute-start(bf16[64,4096]{1,0:T(8,128)(2,1)S(1)} %bitcast.108), channel_id=1, source_target_pairs={{0,128},{1,129},{2,130},{3,131},{4,132},{5,133},{6,134},{7,135},{8... | collective-permute-start | bytes 1572872 | tf_op jit(solution)/shard_map/ppermute | solution.py:15
Sparse Core Ops, SparseCore 0:
  11.0 124.9 all-gather.2
  139.5 120.6 all-gather.4
where the time goes:
time: 464 us; the launch traced here: 462 us
  waiting for transfers between devices  329 us (71%)
  local copies, waits for them, and re-layouts  49.6 us (11%)
  matrix products  36.7 us (8%)
  other arithmetic  29 us (6%)
  between operations  13.6 us (3%)
    all_gather x1, waiting for transfers between devices, body(): lax.all_gather(key_rows, 'ctx', axis=1, tiled=True)  126 us
    all_gather x1, waiting for transfers between devices, body(): lax.all_gather(rows_of_value, 'ctx', axis=1, tiled=True)  112 us
    ppermute x1, waiting for transfers between devices, from_behind(): lax.ppermute(value, axis, [(source, source + steps) for source in range(i...  89.6 us
    while x4, local copies, waits for them, and re-layouts, attend(): lax.fori_loop(0, total_rows // width_of_block, loop_body, start_state)  24.3 us
    dot_general x16, matrix products, compute(): jnp.einsum('jgqk,kjd->qjgd', weights.astype(jnp.bfloat16), value_four, pr...  24.2 us
    reduce_sum x16, other arithmetic, compute(): new_sum = row_sum * rescale + jnp.sum(weights, axis=-1)  20.8 us
    dynamic_slice x16, local copies, waits for them, and re-layouts, loop_body(): lax.dynamic_slice_in_dim(gathered[0][0], first_row_index, width_of_block, 0)  20.4 us
    dot_general x16, matrix products, compute(): jnp.einsum('qjgd,kjd->jgqk', query_four, key_quad, preferred_element_type...  12.4 us
  transfers between devices with their start and end apart: 3, of which 3 were waited for; matrix products, arithmetic and copies ran while one was open for 3% of the time, Pallas kernels for 0%

commit v1 on v0

v1 whole, which is shorter than its diff:
```python
import math

import jax
import jax.numpy as jnp
from jax import lax
from jax.experimental import pallas as pl
from jax.experimental.pallas import tpu as pltpu
from jax.sharding import PartitionSpec as P

MESH = pl.DeviceIdType.MESH
HEAD = 128
NX, NY, NZ = 4, 4, 8
GROUPS = NY * NZ
LOG2_SCALE = math.log2(math.e) / math.sqrt(HEAD)
MASKED = -1e30
KEY_TILE = 512
ROW_TILE = 256


def ring_events(na, nb):
    def offsets(n):
        return [0] + [s * d for d in range(1, n // 2) for s in (1, -1)] + [n // 2]

    events = [(a, b) for a in offsets(na) for b in offsets(nb)]
    return sorted(events, key=lambda e: (abs(e[0]) + abs(e[1]), abs(e[1])))


def here():
    section = lax.axis_index("section")
    ctx = lax.axis_index("ctx")
    return section, ctx, ctx // NX, ctx % NX


def greet(partners):
    barrier = pltpu.get_barrier_semaphore()
    for device in partners:
        pl.semaphore_signal(barrier, inc=1, device_id=device, device_id_type=MESH)
    pl.semaphore_wait(barrier, len(partners))


def remote(src, dst, send_sem, recv_sem, device):
    return pltpu.make_async_remote_copy(
        src_ref=src, dst_ref=dst, send_sem=send_sem, recv_sem=recv_sem,
        device_id=device, device_id_type=MESH,
    )


def group_partner(section, group, x, step):
    other = lax.rem(section * NX + x + step, 2 * NX)
    return other // NX, other % NX, (other // NX, group * NX + other % NX)


def gather_kernel(q_ref, k_ref, v_ref, qx_ref, kv_ref, q_send, q_recv, x_send, x_recv,
                  ring_send, ring_recv, sib_send, sib_recv, own_sem):
    section, ctx, group, x = here()
    y, z = group // NZ, group % NZ

    def at(y_at, z_at):
        return (section, (lax.rem(y_at + NY, NY) * NZ + lax.rem(z_at + NZ, NZ)) * NX + x)

    partners = [group_partner(section, group, x, step)[2] for step in range(1, 2 * NX)]
    greet(partners + [at(y + 1, z), at(y - 1, z), at(y, z + 1), at(y, z - 1)])

    exchanged = []
    for step in range(1, NX):
        x_to = lax.rem(x + step, NX)
        columns = pl.ds(pl.multiple_of(x_to * HEAD, HEAD), HEAD)
        for which, ref in ((0, k_ref), (1, v_ref)):
            copy = remote(
                ref.at[0, :, columns], kv_ref.at[section, group, x, which],
                x_send.at[step - 1, which], x_recv.at[step - 1, which],
                (section, group * NX + x_to),
            )
            copy.start()
            exchanged.append(copy)
    own = []
    columns = pl.ds(pl.multiple_of(x * HEAD, HEAD), HEAD)
    for which, ref in ((0, k_ref), (1, v_ref)):
        own.append(pltpu.make_async_copy(
            ref.at[0, :, columns], kv_ref.at[section, group, x, which], own_sem.at[which]))
    own.append(pltpu.make_async_copy(
        q_ref.at[0, :, pl.ds(pl.multiple_of(x * 1024 + section * 512, 512), 512)],
        qx_ref.at[section, x], own_sem.at[2]))
    for copy in own:
        copy.start()
    moved = []
    for step in range(1, 2 * NX):
        core_to, x_to, device = group_partner(section, group, x, step)
        copy = remote(
            q_ref.at[0, :, pl.ds(pl.multiple_of(x_to * 1024 + core_to * 512, 512), 512)],
            qx_ref.at[section, x], q_send.at[step - 1], q_recv.at[step - 1], device,
        )
        copy.start()
        moved.append(copy)
    for copy in own:
        copy.wait()
    for copy in exchanged:
        copy.wait_recv()

    def rings(na, nb, z_first):
        index = {e: i for i, e in enumerate(ring_events(na, nb))}
        sends = []

        def chunk(a, b):
            y_from, z_from = (y - b, z - a) if z_first else (y - a, z - b)
            return lax.rem(y_from + NY, NY) * NZ + lax.rem(z_from + NZ, NZ)

        def neighbour(da, db):
            return at(y + db, z + da) if z_first else at(y + da, z + db)

        def part(g, half):
            if half is None:
                return kv_ref.at[section, g]
            return kv_ref.at[section, g, pl.ds(2 * half, 2)]

        def copies(g, event, half, device):
            slot = (index[event], 1 if half == 1 else 0)
            piece = part(g, half)
            return remote(piece, piece, ring_send.at[slot], ring_recv.at[slot], device)

        def send(g, event, half, da, db):
            copy = copies(g, event, half, neighbour(da, db))
            copy.start()
            sends.append(copy)

        def halves(d, n):
            return d == n // 2

        siblings = []
        for event, i in index.items():
            a, b = event
            g = chunk(a, b)
            if event != (0, 0):
                if (b != 0 and halves(b, nb)) or (b == 0 and halves(a, na)):
                    for half in (0, 1):
                        copies(g, event, half, at(y, z + 1)).wait_recv()
                else:
                    copies(g, event, None, at(y, z + 1)).wait_recv()
            if b == 0 and not halves(a, na):
                for sign in (1, -1):
                    if a * sign < 0:
                        continue
                    to = a + sign
                    if abs(to) == na // 2:
                        send(g, (na // 2, 0), 0 if sign > 0 else 1, sign, 0)
                    else:
                        send(g, (to, 0), None, sign, 0)
            if not (b != 0 and halves(b, nb)):
                for sign in (1, -1):
                    if b * sign < 0:
                        continue
                    to = b + sign
                    if abs(to) == nb // 2:
                        send(g, (a, nb // 2), 0 if sign > 0 else 1, 0, sign)
                    else:
                        send(g, (a, to), None, 0, sign)
            copy = remote(kv_ref.at[section, g], kv_ref.at[section, g], sib_send.at[i],
                          sib_recv.at[i], (1 - section, ctx))
            copy.start()
            siblings.append(copy)
        for copy in siblings:
            copy.wait_recv()
        for copy in sends + siblings:
            copy.wait_send()

    @pl.when(section == 0)
    def _():
        rings(NZ, NY, True)

    @pl.when(section == 1)
    def _():
        rings(NY, NZ, False)

    for copy in moved:
        copy.wait()
    for copy in exchanged:
        copy.wait_send()


def gather(queries, keys, values):
    rows = queries.shape[1]
    dma = pltpu.SemaphoreType.DMA
    any_spec = pl.BlockSpec(memory_space=pl.ANY)
    return pl.pallas_call(
        gather_kernel,
        out_shape=(
            jax.ShapeDtypeStruct((2, NX, rows, 4 * HEAD), jnp.bfloat16),
            jax.ShapeDtypeStruct((2, GROUPS, NX, 2, rows, HEAD), jnp.bfloat16),
        ),
        in_specs=[any_spec] * 3,
        out_specs=(any_spec, any_spec),
        scratch_shapes=[
            dma((7,)), dma((7,)), dma((3, 2)), dma((3, 2)), dma((32, 2)), dma((32, 2)),
            dma((32,)), dma((32,)), dma((3,)),
        ],
        compiler_params=pltpu.CompilerParams(collective_id=0, has_side_effects=True),
    )(queries, keys, values)


def attend_kernel(qx_ref, kv_hbm, bias_ref, hot_ref, gain_ref, o_ref, kv_ref, qa, m_s, acc_s, sem):
    group = lax.axis_index("ctx") // NX
    loads = [pltpu.make_async_copy(kv_hbm.at[l], kv_ref.at[l], sem.at[l]) for l in range(2)]
    for copy in loads:
        copy.start()

    def widen(v):
        return jnp.concatenate([v, jnp.ones(v.shape, jnp.bfloat16)], axis=1)

    def product(q, k):
        return lax.dot_general(q, k, (((1,), (1,)), ((), ())), preferred_element_type=jnp.float32)

    for layer in range(2):
        loads[layer].wait()
        own_k = kv_ref[layer, group, :, 0].reshape(256, HEAD)
        own_v = widen(kv_ref[layer, group, :, 1].reshape(256, HEAD))
        for x in range(NX):
            rows = pl.ds(x * ROW_TILE, ROW_TILE)
            q = qx_ref[layer, x]
            if layer == 1:
                q = (q.astype(jnp.float32)
                     + gain_ref[...] * o_ref[0, x].astype(jnp.float32)).astype(jnp.bfloat16)
            q = jnp.concatenate([q[:, h * HEAD:(h + 1) * HEAD] for h in range(4)], axis=0)
            for half in range(2):
                qa[half, rows, :HEAD] = q
                qa[half, rows, HEAD:] = bias_ref[x, half]
            s = product(q, own_k)
            r = lax.broadcasted_iota(jnp.int32, s.shape, 0)
            t = lax.broadcasted_iota(jnp.int32, s.shape, 1)
            seen = (t // 32 == x * 2 + (r % 64) // 32) & (t % 32 <= r % 32)
            s = jnp.where(seen, s, MASKED)
            m = jnp.max(s, axis=1, keepdims=True)
            p = jnp.exp2((s - m) * LOG2_SCALE).astype(jnp.bfloat16)
            acc_s[rows, :] = jnp.dot(p, own_v, preferred_element_type=jnp.float32)
            m_s[rows, :] = jnp.broadcast_to(m, (ROW_TILE, HEAD))

        def step(j, _):
            per = KEY_TILE // 256
            k = kv_ref[layer, pl.ds(j * per, per), :, 0].reshape(KEY_TILE, HEAD)
            v = widen(kv_ref[layer, pl.ds(j * per, per), :, 1].reshape(KEY_TILE, HEAD))
            tiles = 4096 // KEY_TILE
            hot = hot_ref[pl.ds(pl.multiple_of(lax.rem(j, tiles) * KEY_TILE, KEY_TILE), KEY_TILE), :]
            k = jnp.concatenate([k, hot], axis=1)
            for x in range(1024 // ROW_TILE):
                rows = pl.ds(x * ROW_TILE, ROW_TILE)
                s = product(qa[j // tiles, rows, :], k)
                m_old = m_s[rows, :]
                m_new = jnp.maximum(m_old, jnp.max(s, axis=1, keepdims=True))
                a = jnp.exp2((m_old - m_new) * LOG2_SCALE)
                wide = jnp.concatenate([m_new] * (KEY_TILE // HEAD), axis=1)
                p = jnp.exp2((s - wide) * LOG2_SCALE).astype(jnp.bfloat16)
                acc_s[rows, :] = (acc_s[rows, :] * jnp.concatenate([a, a], axis=1)
                                  + jnp.dot(p, v, preferred_element_type=jnp.float32))
                m_s[rows, :] = m_new
            return 0

        lax.fori_loop(0, 8192 // KEY_TILE, step, 0)
        for x in range(NX):
            rows = pl.ds(x * ROW_TILE, ROW_TILE)
            out = (acc_s[rows, :HEAD] / acc_s[rows, HEAD:]).astype(jnp.bfloat16)
            o_ref[layer, x] = jnp.concatenate([out[h * 64:(h + 1) * 64] for h in range(4)], axis=1)


def attend(qx, kv, bias, hot, gain):
    vmem = pl.BlockSpec(memory_space=pltpu.VMEM)
    return pl.pallas_call(
        attend_kernel,
        out_shape=jax.ShapeDtypeStruct(qx.shape, jnp.bfloat16),
        in_specs=[vmem, pl.BlockSpec(memory_space=pl.ANY), vmem, vmem, vmem],
        out_specs=vmem,
        scratch_shapes=[
            pltpu.VMEM(kv.shape, jnp.bfloat16),
            pltpu.VMEM((2, 1024, 2 * HEAD), jnp.bfloat16),
            pltpu.VMEM((1024, HEAD), jnp.float32),
            pltpu.VMEM((1024, 2 * HEAD), jnp.float32),
            pltpu.SemaphoreType.DMA((2,)),
        ],
        compiler_params=pltpu.CompilerParams(vmem_limit_bytes=60 * 2**20),
    )(qx, kv, bias, hot, gain)


def return_kernel(o_ref, out_ref, send, recv, own_sem):
    section, ctx, group, x = here()
    greet([group_partner(section, group, x, step)[2] for step in range(1, 2 * NX)])
    columns = pl.ds(pl.multiple_of(x * 1024 + section * 512, 512), 512)
    copies = []
    for step in range(1, 2 * NX):
        layer, x_to, device = group_partner(section, group, x, step)
        copies.append(remote(o_ref.at[layer, x_to], out_ref.at[0, :, columns],
                             send.at[step - 1], recv.at[step - 1], device))
    for copy in copies:
        copy.start()
    own = pltpu.make_async_copy(o_ref.at[section, x], out_ref.at[0, :, columns], own_sem)
    own.start()
    own.wait()
    for copy in copies:
        copy.wait()


def give_back(o, rows):
    dma = pltpu.SemaphoreType.DMA
    any_spec = pl.BlockSpec(memory_space=pl.ANY)
    return pl.pallas_call(
        return_kernel,
        out_shape=jax.ShapeDtypeStruct((1, rows, 4096), jnp.bfloat16),
        in_specs=[any_spec],
        out_specs=any_spec,
        scratch_shapes=[dma((7,)), dma((7,)), dma],
        compiler_params=pltpu.CompilerParams(collective_id=1, has_side_effects=True),
    )(o)


def body(queries, key_rows, rows_of_value, query_gain, block_order):
    section, ctx, group, x = here()
    qx, kv = gather(queries, key_rows, rows_of_value)
    own = lax.dynamic_slice_in_dim(block_order, group * 8, 8, 0)
    hidden = block_order[None, :] >= own[:, None]
    bias = jnp.where(hidden, MASKED, 0.0).astype(jnp.bfloat16).reshape(4, 2, 2, 128)
    bias = jnp.transpose(bias, (0, 2, 1, 3))
    bias = jnp.broadcast_to(bias[:, :, None, :, None, :], (4, 2, 4, 2, 32, 128)).reshape(4, 2, 256, 128)
    key_block = lax.broadcasted_iota(jnp.int32, (4096, 128), 0) // 32
    hot = (key_block == lax.broadcasted_iota(jnp.int32, (4096, 128), 1)).astype(jnp.bfloat16)
    gain = lax.dynamic_slice_in_dim(query_gain, x * 1024 + section * 512, 512, 0)[None, :]
    o = attend(qx, kv, bias, hot, gain)
    return give_back(o, queries.shape[1])


def solution(mesh):
    placed = (
        P("section", "ctx", None),
        P("section", "ctx", None),
        P("section", "ctx", None),
        P(),
        P(),
    )
    return jax.shard_map(
        body, mesh=mesh, in_specs=placed, out_specs=P("section", "ctx", None), check_vma=False
    )
```

time: 464 us -> 108 us (0.23)
  waiting for transfers between devices: 329 us -> 0 us
  Pallas kernels: 0 us -> 97.1 us
  local copies, waits for them, and re-layouts: 49.6 us -> 4.93 us
  matrix products: 36.7 us -> 0 us
  other arithmetic: 29 us -> 5.41 us
  between operations: 13.6 us -> 0.04 us
    all_gather x2 -> x0, waiting for transfers between devices: 238 us -> none  [the longest x1 126 us: body(): lax.all_gather(key_rows, 'ctx', axis=1, tiled=True)]
    pallas_call x0 -> x3, Pallas kernels: none -> 97.1 us  [the longest x1 47.4 us: gather(): pl.pallas_call(gather_kernel, out_shape=(jax.ShapeDtypeStruct((2, NX, row...]
    ppermute x1 -> x0, waiting for transfers between devices: 89.6 us -> none  [from_behind(): lax.ppermute(value, axis, [(source, source + steps) for source in range(i...]
    dot_general x32 -> x0, matrix products: 36.7 us -> none  [the longest x16 24.2 us: compute(): jnp.einsum('jgqk,kjd->qjgd', weights.astype(jnp.bfloat16), value_four, pr...]
    reduce_sum x33 -> x0, other arithmetic: 25.4 us -> none  [the longest x16 20.8 us: compute(): new_sum = row_sum * rescale + jnp.sum(weights, axis=-1)]
    while x4 -> x0, local copies, waits for them, and re-layouts: 24.3 us -> none  [attend(): lax.fori_loop(0, total_rows // width_of_block, loop_body, start_state)]
    dynamic_slice x16 -> x2, local copies, waits for them, and re-layouts: 20.4 us -> 2.1 us  [the longest x1 1.34 us: body(): lax.dynamic_slice_in_dim(query_gain, x * 1024 + section * 512, 512, 0)]
    convert_element_type x1 -> x2, other arithmetic: 0.35 us -> 5.39 us  [the longest x1 4.64 us: body(): (key_block == lax.broadcasted_iota(jnp.int32, (4096, 128), 1)).astype(jnp...]
  transfers between devices with their start and end apart: 3 -> 0, of which waited for: 3 -> 0; matrix products, arithmetic and copies ran while one was open for 3% -> 0% of each run, Pallas kernels for 0% -> 0%
where the time goes in v1:
time: 108 us; the launch traced here: 107 us
  Pallas kernels  97.1 us (90%)
  other arithmetic  5.41 us (5%)
  local copies, waits for them, and re-layouts  4.93 us (5%)
    pallas_call x1, Pallas kernels, gather(): pl.pallas_call(gather_kernel, out_shape=(jax.ShapeDtypeStruct((2, NX, row...  47.4 us
    pallas_call x1, Pallas kernels, attend(): pl.pallas_call(attend_kernel, out_shape=jax.ShapeDtypeStruct(qx.shape, jn...  39.4 us
    pallas_call x1, Pallas kernels, give_back(): pl.pallas_call(return_kernel, out_shape=jax.ShapeDtypeStruct((1, rows, 40...  10.3 us
    convert_element_type x1, other arithmetic, body(): (key_block == lax.broadcasted_iota(jnp.int32, (4096, 128), 1)).astype(jnp...  4.64 us

profile of v1, /device:TPU:1, one launch (start us, length us, event | category | flops | bytes accessed | tf_op | source)
XLA Modules:
  0.0 107.4 jit_solution(15724917302874250613)
XLA Ops:
  0.0 0.8 dynamic_slice.6
  0.8 1.3 %dynamic_slice.7 = f32[512]{0:T(512)} dynamic-slice(f32[4096]{0:T(1024)} %param.8, s32[]{:T(128)S(6)} %select_n.33), dynamic_slice_sizes={512} | dynamic-slice | bytes 4100 | tf_op jit(solution)/shard_map/dynamic_slice | solution.py:322
  2.1 0.1 ge.21
  2.2 0.8 fusion.4
  3.0 0.9 broadcast_in_dim.21
  3.8 4.6 %fusion.hot_ref = bf16[4096,128]{1,0:T(8,128)(2,1)} fusion(s32[4096]{0:T(1024)S(1)} %get-tuple-element.9, s32[4096]{0:T(1024)S(1)} %get-tuple-element.10, pred[4096]{0:T(1024)(128)(4,1)S(1)} %fusion.3), kind=kLoop, calls=%fused_computation.1 | loop fusion | flops 1572864 | bytes 1085440 | tf_op jit(solution)/shard_map/convert_element_type | solution.py:321
  8.5 47.4 %shard_map.55 = (bf16[2,4,64,512]{3,2,1,0:T(8,128)(2,1)}, bf16[2,32,4,2,64,128]{5,4,3,2,1,0:T(8,128)(2,1)}) custom-call(bf16[1,64,4096]{2,1,0:T(8,128)(2,1)} %q_ref.1, bf16[1,64,512]{2,1,0:T(8,128)(2,1)} %k_ref.1, bf16[1,64,512]{2,1,0:T(8,128)(2,1)} %v_ref.1), custom_call_target="tpu_custom_call" | custom-call | tf_op jit(solution)/shard_map/pallas_call | solution.py:184
  55.9 39.4 %shard_map.56.o_ref = bf16[2,4,64,512]{3,2,1,0:T(8,128)(2,1)} custom-call(bf16[2,4,64,512]{3,2,1,0:T(8,128)(2,1)} %get-tuple-element.7.qx_ref, bf16[2,32,4,2,64,128]{5,4,3,2,1,0:T(8,128)(2,1)} %get-tuple-element.8.kv_hbm, bf16[4,2,256,128]{3,2,1,0:T(8,128)(2,1)} %bitcast.3, bf16[4096,128]{1,0:T(8,128)(2,1)} %fusion.hot_ref, f32[1,512]{1,0:T(1,128)} %bitcast.4), custom_call_target="tpu_custom_call" | custom-call | tf_op jit(solution)/shard_map/pallas_call | solution.py:265
  95.3 10.3 %shard_map.57 = bf16[1,64,4096]{2,1,0:T(8,128)(2,1)} custom-call(bf16[2,4,64,512]{3,2,1,0:T(8,128)(2,1)} %shard_map.56.o_ref), custom_call_target="tpu_custom_call" | custom-call | tf_op jit(solution)/shard_map/pallas_call | solution.py:302
  105.6 1.9 %copy.7 = bf16[1,64,4096]{2,1,0:T(8,128)(2,1)} copy(bf16[1,64,4096]{2,1,0:T(8,128)(2,1)} %shard_map.57) | data formatting | bytes 1048576
  (2 shorter events, 0.0 us)

commit v2 on v1

v2 whole, which is shorter than its diff:
```python
import math

import jax
import jax.numpy as jnp
from jax import lax
from jax.experimental import pallas as pl
from jax.experimental.pallas import tpu as pltpu
from jax.sharding import PartitionSpec as P

MESH = pl.DeviceIdType.MESH
HEAD = 128
NX, NY, NZ = 4, 4, 8
GROUPS = NY * NZ
LOG2_SCALE = math.log2(math.e) / math.sqrt(HEAD)
MASKED = -1e30
CHUNK = 256
ROW_TILE = 256


def ring_events(na, nb):
    def offsets(n):
        return [0] + [s * d for d in range(1, n // 2) for s in (1, -1)] + [n // 2]

    events = [(a, b) for a in offsets(na) for b in offsets(nb)]
    return sorted(events, key=lambda e: (abs(e[0]) + abs(e[1]), abs(e[1])))


def here():
    section = lax.axis_index("section")
    ctx = lax.axis_index("ctx")
    return section, ctx, ctx // NX, ctx % NX


def greet(partners):
    barrier = pltpu.get_barrier_semaphore()
    for device in partners:
        pl.semaphore_signal(barrier, inc=1, device_id=device, device_id_type=MESH)
    pl.semaphore_wait(barrier, len(partners))


def remote(src, dst, send_sem, recv_sem, device):
    return pltpu.make_async_remote_copy(
        src_ref=src, dst_ref=dst, send_sem=send_sem, recv_sem=recv_sem,
        device_id=device, device_id_type=MESH,
    )


def group_partner(section, group, x, step):
    other = lax.rem(section * NX + x + step, 2 * NX)
    return other // NX, other % NX, (other // NX, group * NX + other % NX)


def layer_kernel(q_ref, k_ref, v_ref, gain_ref, order_ref, order_smem, out_ref,
                 kv, qx, hot, qa, m_s, acc_s, o_s, q_send, q_recv, x_send, x_recv,
                 ring_send, ring_recv, sib_send, sib_recv, own_sem, out_send, out_recv, out_own):
    section, ctx, group, x = here()
    y, z = group // NZ, group % NZ

    def at(y_at, z_at):
        return (section, (lax.rem(y_at + NY, NY) * NZ + lax.rem(z_at + NZ, NZ)) * NX + x)

    partners = [group_partner(section, group, x, step)[2] for step in range(1, 2 * NX)]
    greet(partners + [at(y + 1, z), at(y - 1, z), at(y, z + 1), at(y, z - 1)])

    exchanged = []
    for step in range(1, NX):
        x_to = lax.rem(x + step, NX)
        columns = pl.ds(pl.multiple_of(x_to * HEAD, HEAD), HEAD)
        for which, ref in ((0, k_ref), (1, v_ref)):
            copy = remote(
                ref.at[0, :, columns], kv.at[section, group, x, which],
                x_send.at[step - 1, which], x_recv.at[step - 1, which],
                (section, group * NX + x_to),
            )
            copy.start()
            exchanged.append(copy)
    own = []
    columns = pl.ds(pl.multiple_of(x * HEAD, HEAD), HEAD)
    for which, ref in ((0, k_ref), (1, v_ref)):
        own.append(pltpu.make_async_copy(
            ref.at[0, :, columns], kv.at[section, group, x, which], own_sem.at[which]))
    own.append(pltpu.make_async_copy(
        q_ref.at[0, :, pl.ds(pl.multiple_of(x * 1024 + section * 512, 512), 512)],
        qx.at[section, x], own_sem.at[2]))
    for copy in own:
        copy.start()
    moved = []
    for step in range(1, 2 * NX):
        core_to, x_to, device = group_partner(section, group, x, step)
        copy = remote(
            q_ref.at[0, :, pl.ds(pl.multiple_of(x_to * 1024 + core_to * 512, 512), 512)],
            qx.at[section, x], q_send.at[step - 1], q_recv.at[step - 1], device,
        )
        copy.start()
        moved.append(copy)
    for copy in own[:2]:
        copy.wait()
    for copy in exchanged:
        copy.wait_recv()

    def sibling_copy(layer, g, i):
        return remote(kv.at[layer, g], kv.at[layer, g], sib_send.at[i], sib_recv.at[i],
                      (1 - section, ctx))

    class Rings:
        def __init__(self, na, nb, z_first):
            self.na, self.nb, self.z_first = na, nb, z_first
            self.events = ring_events(na, nb)
            self.index = {e: i for i, e in enumerate(self.events)}

        def chunk(self, a, b):
            y_from, z_from = (y - b, z - a) if self.z_first else (y - a, z - b)
            return lax.rem(y_from + NY, NY) * NZ + lax.rem(z_from + NZ, NZ)

        def copy(self, g, event, half, da=0, db=1):
            slot = (self.index[event], 1 if half == 1 else 0)
            piece = kv.at[section, g] if half is None else kv.at[section, g, pl.ds(2 * half, 2)]
            device = at(y + db, z + da) if self.z_first else at(y + da, z + db)
            return remote(piece, piece, ring_send.at[slot], ring_recv.at[slot], device)

        def onward(self, event):
            a, b = event
            far_a, far_b = self.na // 2, self.nb // 2
            passed = []
            for sign in (1, -1):
                if b == 0 and a != far_a and a * sign >= 0:
                    to = a + sign
                    if abs(to) == far_a:
                        passed.append(((far_a, 0), 0 if sign > 0 else 1, sign, 0))
                    else:
                        passed.append(((to, 0), None, sign, 0))
            for sign in (1, -1):
                if b != far_b and b * sign >= 0:
                    to = b + sign
                    if abs(to) == far_b:
                        passed.append(((a, far_b), 0 if sign > 0 else 1, 0, sign))
                    else:
                        passed.append(((a, to), None, 0, sign))
            return passed

        def handle(self, i):
            a, b = event = self.events[i]
            g = self.chunk(a, b)
            if i:
                split = b == self.nb // 2 or (b == 0 and a == self.na // 2)
                for half in (0, 1) if split else (None,):
                    self.copy(g, event, half).wait_recv()
            for to, half, da, db in self.onward(event):
                self.copy(g, to, half, da, db).start()
            sibling_copy(section, g, i).start()

        def finish(self):
            for i, event in enumerate(self.events):
                g = self.chunk(*event)
                for to, half, da, db in self.onward(event):
                    self.copy(g, to, half, da, db).wait_send()
                sibling_copy(section, g, i).wait_send()

    first, second = Rings(NZ, NY, True), Rings(NY, NZ, False)

    def advance(indices):
        @pl.when(section == 0)
        def _():
            for i in indices:
                first.handle(i)

        @pl.when(section == 1)
        def _():
            for i in indices:
                second.handle(i)
            for i in indices:
                sibling_copy(0, first.chunk(*first.events[i]), i).wait_recv()

    def arrived(i):
        a, b = first.events[0]
        for n, event in enumerate(first.events[1:], 1):
            a, b = jnp.where(i == n, event[0], a), jnp.where(i == n, event[1], b)
        return first.chunk(a, b)

    advance([0])

    def fill_hot(i, _):
        block = lax.shift_right_logical(lax.broadcasted_iota(jnp.int32, (CHUNK, HEAD), 0), 5)
        lane = lax.broadcasted_iota(jnp.int32, (CHUNK, HEAD), 1)
        rows = pl.ds(pl.multiple_of(i * CHUNK, CHUNK), CHUNK)
        hot[rows, :] = jnp.where(block + i * 8 == lane, 1.0, 0.0).astype(jnp.bfloat16)
        return 0

    lax.fori_loop(0, 16, fill_hot, 0)
    for block in range(8):
        mine = order_smem[group * 8 + block]
        for half in range(2):
            order = jnp.broadcast_to(order_ref[:, half * HEAD:(half + 1) * HEAD], (32, HEAD))
            bias = jnp.where(order >= mine, MASKED, 0.0).astype(jnp.bfloat16)
            for h in range(4):
                qa[half, pl.ds(block // 2 * 256 + h * 64 + block % 2 * 32, 32), HEAD:] = bias
    own[2].wait()
    for copy in moved:
        copy.wait()
    for copy in exchanged:
        copy.wait_send()

    def widen(v):
        return jnp.concatenate([v, jnp.ones(v.shape, jnp.bfloat16)], axis=1)

    def product(q, k):
        return lax.dot_general(q, k, (((1,), (1,)), ((), ())), preferred_element_type=jnp.float32)

    def begin(layer):
        own_k = kv[layer, group, :, 0].reshape(CHUNK, HEAD)
        own_v = widen(kv[layer, group, :, 1].reshape(CHUNK, HEAD))
        for xs in range(NX):
            rows = pl.ds(xs * ROW_TILE, ROW_TILE)
            q = qx[layer, xs]
            if layer == 1:
                gain = gain_ref[:, pl.ds(pl.multiple_of(x * 1024 + section * 512, 512), 512)]
                q = (q.astype(jnp.float32)
                     + gain * o_s[0, xs].astype(jnp.float32)).astype(jnp.bfloat16)
            q = jnp.concatenate([q[:, h * HEAD:(h + 1) * HEAD] for h in range(4)], axis=0)
            for half in range(2):
                qa[half, rows, :HEAD] = q
            s = product(q, own_k)
            r = lax.broadcasted_iota(jnp.int32, s.shape, 0)
            t = lax.broadcasted_iota(jnp.int32, s.shape, 1)
            seen = (t // 32 == xs * 2 + (r % 64) // 32) & (t % 32 <= r % 32)
            s = jnp.where(seen, s, MASKED)
            m = jnp.max(s, axis=1, keepdims=True)
            p = jnp.exp2((s - m) * LOG2_SCALE).astype(jnp.bfloat16)
            acc_s[rows, :] = jnp.dot(p, own_v, preferred_element_type=jnp.float32)
            m_s[rows, :] = jnp.broadcast_to(m, (ROW_TILE, HEAD))

    def fold(layer, chunks):
        keys, values = [], []
        for g in chunks:
            k = kv[layer, g, :, 0].reshape(CHUNK, HEAD)
            rows = pl.ds(pl.multiple_of(lax.rem(g, 16) * CHUNK, CHUNK), CHUNK)
            keys.append(jnp.concatenate([k, hot[rows, :]], axis=1))
            values.append(kv[layer, g, :, 1].reshape(CHUNK, HEAD))
        v = widen(jnp.concatenate(values, axis=0))
        for xs in range(NX):
            rows = pl.ds(xs * ROW_TILE, ROW_TILE)
            s = jnp.concatenate(
                [product(qa[g // 16, rows, :], k) for g, k in zip(chunks, keys)], axis=1)
            m_old = m_s[rows, :]
            m_new = jnp.maximum(m_old, jnp.max(s, axis=1, keepdims=True))
            a = jnp.exp2((m_old - m_new) * LOG2_SCALE)
            wide = jnp.concatenate([m_new] * (s.shape[1] // HEAD), axis=1)
            p = jnp.exp2((s - wide) * LOG2_SCALE).astype(jnp.bfloat16)
            acc_s[rows, :] = (acc_s[rows, :] * jnp.concatenate([a, a], axis=1)
                              + jnp.dot(p, v, preferred_element_type=jnp.float32))
            m_s[rows, :] = m_new

    back = pl.ds(pl.multiple_of(x * 1024 + section * 512, 512), 512)

    def return_copy(layer, k):
        x_to = lax.rem(x + k, NX)
        return remote(o_s.at[layer, x_to], out_ref.at[0, :, back], out_send.at[layer, k],
                      out_recv.at[section, k], (layer, group * NX + x_to))

    def own_return():
        return pltpu.make_async_copy(o_s.at[section, x], out_ref.at[0, :, back], out_own)

    def end(layer):
        for xs in range(NX):
            rows = pl.ds(xs * ROW_TILE, ROW_TILE)
            out = (acc_s[rows, :HEAD] / acc_s[rows, HEAD:]).astype(jnp.bfloat16)
            o_s[layer, xs] = jnp.concatenate([out[h * 64:(h + 1) * 64] for h in range(4)], axis=1)

    def send_back(layer):
        for k in range(1, NX):
            return_copy(layer, k).start()

        @pl.when(section != layer)
        def _():
            return_copy(layer, 0).start()

        @pl.when(section == layer)
        def _():
            own_return().start()

    begin(0)

    def step0(j, _):
        for i in range(16):
            @pl.when(j == i)
            def _():
                advance([2 * i, 2 * i + 1] if i else [1])
        fold(0, [arrived(2 * j), arrived(2 * j + 1)])
        return 0

    lax.fori_loop(0, 16, step0, 0)
    end(0)

    @pl.when(section == 0)
    def _():
        for i, event in enumerate(second.events):
            sibling_copy(1, second.chunk(*event), i).wait_recv()

    begin(1)
    send_back(0)

    def step1(j, _):
        fold(1, [2 * j, 2 * j + 1])
        return 0

    lax.fori_loop(0, 16, step1, 0)
    end(1)
    send_back(1)

    @pl.when(section == 0)
    def _():
        first.finish()

    @pl.when(section == 1)
    def _():
        second.finish()

    own_return().wait()
    for core in range(2):
        for k in range(1, NX):
            return_copy(core, k).wait_send()
            remote(o_s.at[0, 0], out_ref.at[0, :, back], out_send.at[core, k],
                   out_recv.at[core, k], (1 - section, ctx)).wait_recv()

        @pl.when(section != core)
        def _():
            return_copy(core, 0).wait_send()
            remote(o_s.at[0, 0], out_ref.at[0, :, back], out_send.at[core, 0],
                   out_recv.at[core, 0], (1 - section, ctx)).wait_recv()


def body(queries, key_rows, rows_of_value, query_gain, block_order):
    rows = queries.shape[1]
    dma = pltpu.SemaphoreType.DMA
    hbm = pl.BlockSpec(memory_space=pl.ANY)
    vmem = pl.BlockSpec(memory_space=pltpu.VMEM)
    return pl.pallas_call(
        layer_kernel,
        out_shape=jax.ShapeDtypeStruct(queries.shape, jnp.bfloat16),
        in_specs=[hbm, hbm, hbm, vmem, vmem, pl.BlockSpec(memory_space=pltpu.SMEM)],
        out_specs=hbm,
        scratch_shapes=[
            pltpu.VMEM((2, GROUPS, NX, 2, rows, HEAD), jnp.bfloat16),
            pltpu.VMEM((2, NX, rows, 4 * HEAD), jnp.bfloat16),
            pltpu.VMEM((4096, HEAD), jnp.bfloat16),
            pltpu.VMEM((2, 1024, 2 * HEAD), jnp.bfloat16),
            pltpu.VMEM((1024, HEAD), jnp.float32),
            pltpu.VMEM((1024, 2 * HEAD), jnp.float32),
            pltpu.VMEM((2, NX, rows, 4 * HEAD), jnp.bfloat16),
            dma((7,)), dma((7,)), dma((3, 2)), dma((3, 2)), dma((32, 2)), dma((32, 2)),
            dma((32,)), dma((32,)), dma((3,)), dma((2, 4)), dma((2, 4)), dma,
        ],
        compiler_params=pltpu.CompilerParams(
            collective_id=0, has_side_effects=True, vmem_limit_bytes=60 * 2**20),
    )(queries, key_rows, rows_of_value, query_gain[None, :], block_order[None, :], block_order)


def solution(mesh):
    placed = (
        P("section", "ctx", None),
        P("section", "ctx", None),
        P("section", "ctx", None),
        P(),
        P(),
    )
    return jax.shard_map(
        body, mesh=mesh, in_specs=placed, out_specs=P("section", "ctx", None), check_vma=False
    )
```

time: 108 us -> 74.2 us (0.69)
  Pallas kernels: 97.1 us -> 72.1 us
  other arithmetic: 5.41 us -> 0 us
  local copies, waits for them, and re-layouts: 4.93 us -> 1.87 us
    pallas_call x3 -> x1, Pallas kernels: 97.1 us -> 72.1 us  [body(): pl.pallas_call(layer_kernel, out_shape=jax.ShapeDtypeStruct(queries.shape...]
    convert_element_type x2 -> x0, other arithmetic: 5.39 us -> none  [the longest x1 4.64 us: body(): (key_block == lax.broadcasted_iota(jnp.int32, (4096, 128), 1)).astype(jnp...]
    dynamic_slice x2 -> x0, local copies, waits for them, and re-layouts: 2.1 us -> none  [the longest x1 1.34 us: body(): lax.dynamic_slice_in_dim(query_gain, x * 1024 + section * 512, 512, 0)]
where the time goes in v2:
time: 74.2 us; the launch traced here: 73.9 us
  Pallas kernels  72.1 us (97%)
  local copies, waits for them, and re-layouts  1.87 us (3%)
    pallas_call x1, Pallas kernels, body(): pl.pallas_call(layer_kernel, out_shape=jax.ShapeDtypeStruct(queries.shape...  72.1 us
    unnamed x1, local copies, waits for them, and re-layouts  1.87 us

profile of v2, /device:TPU:1, one launch (start us, length us, event | category | flops | bytes accessed | tf_op | source)
XLA Modules:
  0.0 73.9 jit_solution(302005076695569214)
XLA Ops:
  0.0 72.1 %shard_map.55 = bf16[1,64,4096]{2,1,0:T(8,128)(2,1)} custom-call(bf16[1,64,4096]{2,1,0:T(8,128)(2,1)} %q_ref.1, bf16[1,64,512]{2,1,0:T(8,128)(2,1)} %k_ref.1, bf16[1,64,512]{2,1,0:T(8,128)(2,1)} %v_ref.1, f32[1,4096]{1,0:T(1,128)} %bitcast.2, s32[1,256]{1,0:T(1,128)} %bitcast.3, s32[256]{0:T(256)} %order_smem.1), custom_call_target="tpu_custom_call" | custom-call | tf_op jit(solution)/shard_map/pallas_call | solution.py:337
  72.1 1.9 %copy.7 = bf16[1,64,4096]{2,1,0:T(8,128)(2,1)} copy(bf16[1,64,4096]{2,1,0:T(8,128)(2,1)} %shard_map.55) | data formatting | bytes 1048576

commit v3 on v2

--- a/solution.py
+++ b/solution.py
@@ -84,15 +84,34 @@
         qx.at[section, x], own_sem.at[2]))
     for copy in own:
         copy.start()
-    moved = []
-    for step in range(1, 2 * NX):
-        core_to, x_to, device = group_partner(section, group, x, step)
-        copy = remote(
+    def query_copy(core_to, k):
+        x_to = lax.rem(x + k, NX)
+        return remote(
             q_ref.at[0, :, pl.ds(pl.multiple_of(x_to * 1024 + core_to * 512, 512), 512)],
-            qx.at[section, x], q_send.at[step - 1], q_recv.at[step - 1], device,
+            qx.at[section, x], q_send.at[core_to, k], q_recv.at[section, k],
+            (core_to, group * NX + x_to),
         )
-        copy.start()
-        moved.append(copy)
+
+    def send_queries(layer):
+        for core in range(2):
+            for k in range(1, NX):
+                query_copy(core, k).start()
+        query_copy(1 - layer, 0).start()
+
+    def wait_queries(layer):
+        for k in range(1, NX):
+            remote(qx.at[layer, x], qx.at[layer, x], q_send.at[0, k], q_recv.at[layer, k],
+                   (1 - section, ctx)).wait_recv()
+
+        @pl.when(section != layer)
+        def _():
+            remote(qx.at[layer, x], qx.at[layer, x], q_send.at[0, 0], q_recv.at[layer, 0],
+                   (1 - section, ctx)).wait_recv()
+
+    @pl.when(section == 0)
+    def _():
+        send_queries(0)
+
     for copy in own[:2]:
         copy.wait()
     for copy in exchanged:
@@ -195,8 +214,7 @@
             for h in range(4):
                 qa[half, pl.ds(block // 2 * 256 + h * 64 + block % 2 * 32, 32), HEAD:] = bias
     own[2].wait()
-    for copy in moved:
-        copy.wait()
+    wait_queries(0)
     for copy in exchanged:
         copy.wait_send()
 
@@ -229,18 +247,25 @@
             acc_s[rows, :] = jnp.dot(p, own_v, preferred_element_type=jnp.float32)
             m_s[rows, :] = jnp.broadcast_to(m, (ROW_TILE, HEAD))
 
-    def fold(layer, chunks):
-        keys, values = [], []
-        for g in chunks:
-            k = kv[layer, g, :, 0].reshape(CHUNK, HEAD)
-            rows = pl.ds(pl.multiple_of(lax.rem(g, 16) * CHUNK, CHUNK), CHUNK)
-            keys.append(jnp.concatenate([k, hot[rows, :]], axis=1))
-            values.append(kv[layer, g, :, 1].reshape(CHUNK, HEAD))
-        v = widen(jnp.concatenate(values, axis=0))
-        for xs in range(NX):
-            rows = pl.ds(xs * ROW_TILE, ROW_TILE)
-            s = jnp.concatenate(
+    def fold(layer, chunk_groups, tiles):
+        operands = []
+        for chunks in chunk_groups:
+            keys, values = [], []
+            for g in chunks:
+                k = kv[layer, g, :, 0].reshape(CHUNK, HEAD)
+                rows = pl.ds(pl.multiple_of(lax.rem(g, 16) * CHUNK, CHUNK), CHUNK)
+                keys.append(jnp.concatenate([k, hot[rows, :]], axis=1))
+                values.append(kv[layer, g, :, 1].reshape(CHUNK, HEAD))
+            operands.append((chunks, keys, widen(jnp.concatenate(values, axis=0))))
+        items = [(operand, pl.ds(xs * ROW_TILE, ROW_TILE)) for operand in operands for xs in tiles]
+
+        def scores(item):
+            (chunks, keys, _), rows = item
+            return jnp.concatenate(
                 [product(qa[g // 16, rows, :], k) for g, k in zip(chunks, keys)], axis=1)
+
+        def update(item, s):
+            (_, _, v), rows = item
             m_old = m_s[rows, :]
             m_new = jnp.maximum(m_old, jnp.max(s, axis=1, keepdims=True))
             a = jnp.exp2((m_old - m_new) * LOG2_SCALE)
@@ -250,62 +275,78 @@
                               + jnp.dot(p, v, preferred_element_type=jnp.float32))
             m_s[rows, :] = m_new
 
+        s = scores(items[0])
+        for i, item in enumerate(items):
+            later = scores(items[i + 1]) if i + 1 < len(items) else None
+            update(item, s)
+            s = later
+
     back = pl.ds(pl.multiple_of(x * 1024 + section * 512, 512), 512)
 
-    def return_copy(layer, k):
-        x_to = lax.rem(x + k, NX)
-        return remote(o_s.at[layer, x_to], out_ref.at[0, :, back], out_send.at[layer, k],
+    def return_copy(layer, x_to):
+        k = lax.rem(x_to + NX - x, NX)
+        return remote(o_s.at[layer, x_to], out_ref.at[0, :, back], out_send.at[layer, x_to],
                       out_recv.at[section, k], (layer, group * NX + x_to))
 
     def own_return():
         return pltpu.make_async_copy(o_s.at[section, x], out_ref.at[0, :, back], out_own)
 
-    def end(layer):
-        for xs in range(NX):
+    def end(layer, tiles):
+        for xs in tiles:
             rows = pl.ds(xs * ROW_TILE, ROW_TILE)
             out = (acc_s[rows, :HEAD] / acc_s[rows, HEAD:]).astype(jnp.bfloat16)
             o_s[layer, xs] = jnp.concatenate([out[h * 64:(h + 1) * 64] for h in range(4)], axis=1)
 
-    def send_back(layer):
-        for k in range(1, NX):
-            return_copy(layer, k).start()
-
-        @pl.when(section != layer)
+    def send_back(layer, tiles):
+        for x_to in tiles:
+            stays = (section == layer) & (x == x_to)
+
+            @pl.when(jnp.logical_not(stays))
+            def _():
+                return_copy(layer, x_to).start()
+
+            @pl.when(stays)
+            def _():
+                own_return().start()
+
+    begin(0)
+    advance([1, 2, 3])
+
+    def step0(j, _):
+        chunks = [arrived(4 * j + i) for i in range(4)]
+        for half in range(2):
+            fold(0, [chunks], (2 * half, 2 * half + 1))
+            for i in range(7):
+                @pl.when(j == i)
+                def _():
+                    advance([4 * i + 4 + 2 * half, 4 * i + 5 + 2 * half])
+
+        @pl.when((j == 1) & (section == 1))
         def _():
-            return_copy(layer, 0).start()
-
-        @pl.when(section == layer)
-        def _():
-            own_return().start()
-
-    begin(0)
-
-    def step0(j, _):
-        for i in range(16):
-            @pl.when(j == i)
-            def _():
-                advance([2 * i, 2 * i + 1] if i else [1])
-        fold(0, [arrived(2 * j), arrived(2 * j + 1)])
+            send_queries(1)
+
         return 0
 
-    lax.fori_loop(0, 16, step0, 0)
-    end(0)
+    lax.fori_loop(0, 8, step0, 0)
+    end(0, range(NX))
 
     @pl.when(section == 0)
     def _():
         for i, event in enumerate(second.events):
             sibling_copy(1, second.chunk(*event), i).wait_recv()
 
+    wait_queries(1)
     begin(1)
-    send_back(0)
-
-    def step1(j, _):
-        fold(1, [2 * j, 2 * j + 1])
-        return 0
-
-    lax.fori_loop(0, 16, step1, 0)
-    end(1)
-    send_back(1)
+    send_back(0, range(NX))
+
+    for tiles in ((0, 1), (2, 3)):
+        def step1(j, _):
+            fold(1, [[8 * j + 4 * i + c for c in range(4)] for i in range(2)], tiles)
+            return 0
+
+        lax.fori_loop(0, 4, step1, 0)
+        end(1, tiles)
+        send_back(1, tiles)
 
     @pl.when(section == 0)
     def _():
@@ -315,16 +356,23 @@
     def _():
         second.finish()
 
-    own_return().wait()
     for core in range(2):
         for k in range(1, NX):
-            return_copy(core, k).wait_send()
+            query_copy(core, k).wait_send()
+    query_copy(1 - section, 0).wait_send()
+    own_return().wait()
+    for layer in range(2):
+        for x_to in range(NX):
+            @pl.when(jnp.logical_not((section == layer) & (x == x_to)))
+            def _():
+                return_copy(layer, x_to).wait_send()
+    for core in range(2):
+        for k in range(1, NX):
             remote(o_s.at[0, 0], out_ref.at[0, :, back], out_send.at[core, k],
                    out_recv.at[core, k], (1 - section, ctx)).wait_recv()
 
         @pl.when(section != core)
         def _():
-            return_copy(core, 0).wait_send()
             remote(o_s.at[0, 0], out_ref.at[0, :, back], out_send.at[core, 0],
                    out_recv.at[core, 0], (1 - section, ctx)).wait_recv()
 
@@ -347,7 +395,7 @@
             pltpu.VMEM((1024, HEAD), jnp.float32),
             pltpu.VMEM((1024, 2 * HEAD), jnp.float32),
             pltpu.VMEM((2, NX, rows, 4 * HEAD), jnp.bfloat16),
-            dma((7,)), dma((7,)), dma((3, 2)), dma((3, 2)), dma((32, 2)), dma((32, 2)),
+            dma((2, 4)), dma((2, 4)), dma((3, 2)), dma((3, 2)), dma((32, 2)), dma((32, 2)),
             dma((32,)), dma((32,)), dma((3,)), dma((2, 4)), dma((2, 4)), dma,
         ],
         compiler_params=pltpu.CompilerParams(

time: 74.2 us -> 65.9 us (0.89)
  Pallas kernels: 72.1 us -> 63.8 us
    pallas_call x1, Pallas kernels: 72.1 us -> 63.8 us  [body(): pl.pallas_call(layer_kernel, out_shape=jax.ShapeDtypeStruct(queries.shape...]
where the time goes in v3:
time: 65.9 us; the launch traced here: 65.6 us
  Pallas kernels  63.8 us (97%)
  local copies, waits for them, and re-layouts  1.87 us (3%)
    pallas_call x1, Pallas kernels, body(): pl.pallas_call(layer_kernel, out_shape=jax.ShapeDtypeStruct(queries.shape...  63.8 us
    unnamed x1, local copies, waits for them, and re-layouts  1.87 us

profile of v3, /device:TPU:1, one launch (start us, length us, event | category | flops | bytes accessed | tf_op | source)
XLA Modules:
  0.0 65.6 jit_solution(10775058954531018941)
XLA Ops:
  0.0 63.8 %shard_map.55 = bf16[1,64,4096]{2,1,0:T(8,128)(2,1)} custom-call(bf16[1,64,4096]{2,1,0:T(8,128)(2,1)} %q_ref.1, bf16[1,64,512]{2,1,0:T(8,128)(2,1)} %k_ref.1, bf16[1,64,512]{2,1,0:T(8,128)(2,1)} %v_ref.1, f32[1,4096]{1,0:T(1,128)} %bitcast.2, s32[1,256]{1,0:T(1,128)} %bitcast.3, s32[256]{0:T(256)} %order_smem.1), custom_call_target="tpu_custom_call" | custom-call | tf_op jit(solution)/shard_map/pallas_call | solution.py:385
  63.8 1.9 %copy.7 = bf16[1,64,4096]{2,1,0:T(8,128)(2,1)} copy(bf16[1,64,4096]{2,1,0:T(8,128)(2,1)} %shard_map.55) | data formatting | bytes 1048576

commit v4 on v3

--- a/solution.py
+++ b/solution.py
@@ -112,6 +112,22 @@
     def _():
         send_queries(0)
 
+    def fill_hot(i, _):
+        block = lax.shift_right_logical(lax.broadcasted_iota(jnp.int32, (CHUNK, HEAD), 0), 5)
+        lane = lax.broadcasted_iota(jnp.int32, (CHUNK, HEAD), 1)
+        rows = pl.ds(pl.multiple_of(i * CHUNK, CHUNK), CHUNK)
+        hot[rows, :] = jnp.where(block + i * 8 == lane, 1.0, 0.0).astype(jnp.bfloat16)
+        return 0
+
+    lax.fori_loop(0, 16, fill_hot, 0)
+    for block in range(8):
+        mine = order_smem[group * 8 + block]
+        for half in range(2):
+            order = jnp.broadcast_to(order_ref[:, half * HEAD:(half + 1) * HEAD], (32, HEAD))
+            bias = jnp.where(order >= mine, MASKED, 0.0).astype(jnp.bfloat16)
+            for h in range(4):
+                qa[half, pl.ds(block // 2 * 256 + h * 64 + block % 2 * 32, 32), HEAD:] = bias
+
     for copy in own[:2]:
         copy.wait()
     for copy in exchanged:
@@ -190,29 +206,16 @@
             for i in indices:
                 sibling_copy(0, first.chunk(*first.events[i]), i).wait_recv()
 
-    def arrived(i):
-        a, b = first.events[0]
-        for n, event in enumerate(first.events[1:], 1):
-            a, b = jnp.where(i == n, event[0], a), jnp.where(i == n, event[1], b)
-        return first.chunk(a, b)
+    def arrived(j):
+        packed = [[(e[0] + 8) * 16 + e[1] + 8 for e in first.events[c::4]] for c in range(4)]
+        places = [jnp.int32(row[0]) for row in packed]
+        for n in range(1, 8):
+            now = j == n
+            places = [jnp.where(now, row[n], place) for row, place in zip(packed, places)]
+        return [first.chunk(place // 16 - 8, place % 16 - 8) for place in places]
 
     advance([0])
-
-    def fill_hot(i, _):
-        block = lax.shift_right_logical(lax.broadcasted_iota(jnp.int32, (CHUNK, HEAD), 0), 5)
-        lane = lax.broadcasted_iota(jnp.int32, (CHUNK, HEAD), 1)
-        rows = pl.ds(pl.multiple_of(i * CHUNK, CHUNK), CHUNK)
-        hot[rows, :] = jnp.where(block + i * 8 == lane, 1.0, 0.0).astype(jnp.bfloat16)
-        return 0
-
-    lax.fori_loop(0, 16, fill_hot, 0)
-    for block in range(8):
-        mine = order_smem[group * 8 + block]
-        for half in range(2):
-            order = jnp.broadcast_to(order_ref[:, half * HEAD:(half + 1) * HEAD], (32, HEAD))
-            bias = jnp.where(order >= mine, MASKED, 0.0).astype(jnp.bfloat16)
-            for h in range(4):
-                qa[half, pl.ds(block // 2 * 256 + h * 64 + block % 2 * 32, 32), HEAD:] = bias
+    advance([1, 2, 3, 4])
     own[2].wait()
     wait_queries(0)
     for copy in exchanged:
@@ -225,8 +228,6 @@
         return lax.dot_general(q, k, (((1,), (1,)), ((), ())), preferred_element_type=jnp.float32)
 
     def begin(layer):
-        own_k = kv[layer, group, :, 0].reshape(CHUNK, HEAD)
-        own_v = widen(kv[layer, group, :, 1].reshape(CHUNK, HEAD))
         for xs in range(NX):
             rows = pl.ds(xs * ROW_TILE, ROW_TILE)
             q = qx[layer, xs]
@@ -237,10 +238,13 @@
             q = jnp.concatenate([q[:, h * HEAD:(h + 1) * HEAD] for h in range(4)], axis=0)
             for half in range(2):
                 qa[half, rows, :HEAD] = q
+            pair = pl.ds(xs // 2 * 2, 2)
+            own_k = kv[layer, group, pair, 0].reshape(CHUNK // 2, HEAD)
+            own_v = widen(kv[layer, group, pair, 1].reshape(CHUNK // 2, HEAD))
             s = product(q, own_k)
             r = lax.broadcasted_iota(jnp.int32, s.shape, 0)
             t = lax.broadcasted_iota(jnp.int32, s.shape, 1)
-            seen = (t // 32 == xs * 2 + (r % 64) // 32) & (t % 32 <= r % 32)
+            seen = (t // 32 == xs % 2 * 2 + (r % 64) // 32) & (t % 32 <= r % 32)
             s = jnp.where(seen, s, MASKED)
             m = jnp.max(s, axis=1, keepdims=True)
             p = jnp.exp2((s - m) * LOG2_SCALE).astype(jnp.bfloat16)
@@ -310,16 +314,15 @@
                 own_return().start()
 
     begin(0)
-    advance([1, 2, 3])
 
     def step0(j, _):
-        chunks = [arrived(4 * j + i) for i in range(4)]
+        chunks = arrived(j)
         for half in range(2):
             fold(0, [chunks], (2 * half, 2 * half + 1))
             for i in range(7):
                 @pl.when(j == i)
                 def _():
-                    advance([4 * i + 4 + 2 * half, 4 * i + 5 + 2 * half])
+                    advance([e for e in (4 * i + 4 + 2 * half, 4 * i + 5 + 2 * half) if e > 4])
 
         @pl.when((j == 1) & (section == 1))
         def _():

time: 65.9 us -> 65.6 us (level)
  no operation moved by 1% of the time
where the time goes in v4:
time: 65.6 us; the launch traced here: 65.4 us
  Pallas kernels  63.5 us (97%)
  local copies, waits for them, and re-layouts  1.87 us (3%)
    pallas_call x1, Pallas kernels, body(): pl.pallas_call(layer_kernel, out_shape=jax.ShapeDtypeStruct(queries.shape...  63.5 us
    unnamed x1, local copies, waits for them, and re-layouts  1.87 us

profile of v4, /device:TPU:1, one launch (start us, length us, event | category | flops | bytes accessed | tf_op | source)
XLA Modules:
  0.0 65.4 jit_solution(13075314186732753617)
XLA Ops:
  0.0 63.5 %shard_map.55 = bf16[1,64,4096]{2,1,0:T(8,128)(2,1)} custom-call(bf16[1,64,4096]{2,1,0:T(8,128)(2,1)} %q_ref.1, bf16[1,64,512]{2,1,0:T(8,128)(2,1)} %k_ref.1, bf16[1,64,512]{2,1,0:T(8,128)(2,1)} %v_ref.1, f32[1,4096]{1,0:T(1,128)} %bitcast.2, s32[1,256]{1,0:T(1,128)} %bitcast.3, s32[256]{0:T(256)} %order_smem.1), custom_call_target="tpu_custom_call" | custom-call | tf_op jit(solution)/shard_map/pallas_call | solution.py:388
  63.5 1.9 %copy.7 = bf16[1,64,4096]{2,1,0:T(8,128)(2,1)} copy(bf16[1,64,4096]{2,1,0:T(8,128)(2,1)} %shard_map.55) | data formatting | bytes 1048576

commit v5 on v4

--- a/solution.py
+++ b/solution.py
@@ -180,9 +180,9 @@
                 split = b == self.nb // 2 or (b == 0 and a == self.na // 2)
                 for half in (0, 1) if split else (None,):
                     self.copy(g, event, half).wait_recv()
+            sibling_copy(section, g, i).start()
             for to, half, da, db in self.onward(event):
                 self.copy(g, to, half, da, db).start()
-            sibling_copy(section, g, i).start()
 
         def finish(self):
             for i, event in enumerate(self.events):

time: 65.6 us -> 65.6 us (level)
  no operation moved by 1% of the time
where the time goes in v5:
time: 65.6 us; the launch traced here: 65.4 us
  Pallas kernels  63.5 us (97%)
  local copies, waits for them, and re-layouts  1.87 us (3%)
    pallas_call x1, Pallas kernels, body(): pl.pallas_call(layer_kernel, out_shape=jax.ShapeDtypeStruct(queries.shape...  63.5 us
    unnamed x1, local copies, waits for them, and re-layouts  1.87 us

profile of v5, /device:TPU:1, one launch (start us, length us, event | category | flops | bytes accessed | tf_op | source)
XLA Modules:
  0.0 65.4 jit_solution(2640649447923183580)
XLA Ops:
  0.0 63.5 %shard_map.55 = bf16[1,64,4096]{2,1,0:T(8,128)(2,1)} custom-call(bf16[1,64,4096]{2,1,0:T(8,128)(2,1)} %q_ref.1, bf16[1,64,512]{2,1,0:T(8,128)(2,1)} %k_ref.1, bf16[1,64,512]{2,1,0:T(8,128)(2,1)} %v_ref.1, f32[1,4096]{1,0:T(1,128)} %bitcast.2, s32[1,256]{1,0:T(1,128)} %bitcast.3, s32[256]{0:T(256)} %order_smem.1), custom_call_target="tpu_custom_call" | custom-call | tf_op jit(solution)/shard_map/pallas_call | solution.py:388
  63.5 1.9 %copy.7 = bf16[1,64,4096]{2,1,0:T(8,128)(2,1)} copy(bf16[1,64,4096]{2,1,0:T(8,128)(2,1)} %shard_map.55) | data formatting | bytes 1048576
